TPU v7x, 32 devices: a whole 2x2x4 slice. The times are simulated.
32 devices in a mesh: space: 16 (over z, x, core), mem: 2 (over y).
Axes of the slice: x: 2, y: 2, z: 4, core: 2. Of those that a mesh axis runs over, the one named last changes fastest.
Arguments:
- ensemble: bfloat16 [8, 32, 512, 1536], P('mem', None, 'space'), may hold values from -12 to 12
- vector: bfloat16 [32, 512, 1536], P(None, 'space'), may hold values from -6 to 6
- modes: float32 [16, 32], replicated, may hold values from -1 to 1
- legendre: bfloat16 [512, 512, 256], P('space'), may hold values from -0.25 to 0.25
- spectrum: float32 [512, 256], P('space'), may hold values from 0.1 to 1
- truncation: int32 [1], replicated, may hold values from 543 to 702
Outputs:
- covariance_apply: bfloat16 [32, 512, 1536], P(None, 'space')
All inputs are finite; a program needn't handle non-finite values.
Results may differ from a plain program's by a relative error of at most 0.014.
Values may be sent and summed in bfloat16 or wider, within the bound.
A program may use at most 128 MiB of HBM per device.

v0:
```python
import math

import jax
import jax.numpy as jnp
from jax import lax
from jax.sharding import PartitionSpec as P

NMODE = 16
NLON = 1536
M = 512
NDEG = 256


def fourier_table(length, wave_count):
    points = jnp.arange(length, dtype=jnp.int32)
    orders = jnp.arange(wave_count, dtype=jnp.int32)
    phases = points[:, None] * orders[None, :] % length
    angles = phases.astype(jnp.float32) * (2.0 * math.pi / length)
    amplitude = math.sqrt(2.0 / length)
    stacked = jnp.stack([jnp.cos(angles), -jnp.sin(angles)], axis=-1) * amplitude
    return stacked.reshape(length, 2 * wave_count).astype(jnp.bfloat16)


def on_device(ensemble, vector, modes, legendre, spectrum, truncation):
    members = ensemble.shape[0]
    lat_rows = ensemble.shape[2]
    own_waves = legendre.shape[0]
    sources = lax.axis_size("space")
    total_members = members * lax.axis_size("mem")
    highest = lax.Precision.HIGHEST
    fourier = fourier_table(NLON, M)
    product = ensemble.astype(jnp.float32) * vector.astype(jnp.float32)[None]
    projected = jnp.einsum("jl,klac->kjac", modes, product, precision=highest).astype(jnp.bfloat16)
    fields = members * NMODE
    columns = fields * lat_rows
    zonal_parts = lax.dot_general(
        fourier,
        projected.reshape(columns, NLON),
        (((0,), (1,)), ((), ())),
        preferred_element_type=jnp.float32,
    )
    zonal_parts = zonal_parts.astype(jnp.bfloat16).reshape(1, 2 * M, columns)
    first_wave = lax.axis_index("space") * own_waves
    wavenumber = (
        first_wave
        + jnp.arange(own_waves, dtype=jnp.int32)[:, None]
        + jnp.arange(NDEG, dtype=jnp.int32)[None, :]
    )
    factor = jnp.where(wavenumber <= truncation[0], spectrum, jnp.zeros_like(spectrum))
    arrived = lax.all_to_all(zonal_parts, "space", split_axis=1, concat_axis=0, tiled=True)
    arrived = arrived.reshape(sources, own_waves, 2, fields, lat_rows)
    legendre_view = legendre.reshape(own_waves, sources, lat_rows, NDEG)
    harmonic = jnp.einsum(
        "smrfa,msan->mrfn", arrived, legendre_view, preferred_element_type=jnp.float32
    )
    weighted = (harmonic * factor[:, None, None, :]).astype(jnp.bfloat16)
    synthesis = jnp.einsum(
        "mrfn,msan->smrfa", weighted, legendre_view, preferred_element_type=jnp.float32
    )
    synthesis = synthesis.astype(jnp.bfloat16).reshape(sources, 2 * own_waves, columns)
    returned = lax.all_to_all(synthesis, "space", split_axis=0, concat_axis=1, tiled=True)
    spread = lax.dot_general(
        returned.reshape(2 * M, columns),
        fourier,
        (((0,), (1,)), ((), ())),
        preferred_element_type=jnp.float32,
    )
    spread = spread.reshape(members, NMODE, lat_rows, NLON)
    lifted = jnp.einsum("jl,kjac->klac", modes, spread, precision=highest)
    partial_value = jnp.sum(ensemble.astype(jnp.float32) * lifted, axis=0)
    summed = lax.psum(partial_value.astype(jnp.bfloat16), "mem").astype(jnp.float32)
    return (summed / (total_members - 1)).astype(jnp.bfloat16)


def solution(mesh):
    placed = (
        P("mem", None, "space", None),
        P(None, "space", None),
        P(),
        P("space", None, None),
        P("space", None),
        P(),
    )
    return jax.shard_map(
        on_device, mesh=mesh, in_specs=placed, out_specs=P(None, "space", None), check_vma=False
    )
```

profile of v0, /device:TPU:15, one launch (start us, length us, event | category | flops | bytes accessed | tf_op | source)
XLA Modules:
  0.0 603.8 jit_solution(11271373535638854482)
XLA Ops:
  6.5 23.6 %sine_negate_fusion = (f32[1536,512,1]{1,0,2:T(8,128)S(1)}, f32[1536,512,1]{1,0,2:T(8,128)S(1)}) fusion(), kind=kLoop, calls=%fused_computation.23 | loop fusion | flops 7864320 | bytes 6291456 | tf_op jit(solution)/shard_map/neg | solution.py:20
  32.1 19.5 %convert_bitcast_fusion.1 = bf16[4,16,32,1536]{3,1,2,0:T(8,128)(2,1)S(1)} fusion(f32[32,32,1536]{2,0,1:T(8,128)S(1)} %copy.28, bf16[4,32,32,1536]{3,2,1,0:T(8,128)(2,1)S(1)} %copy-done.1, f32[16,32]{1,0:T(8,128)S(1)} %copy-done), kind=kOutput, calls=%fused_computation.13 | convolution fusion | flops 1223688192 | bytes 25167872 | tf_op jit(solution)/shard_map/jl,klac->kjac/dot_general | solution.py:33
  51.5 6.1 %copy.29 = bf16[4,16,32,1536]{3,2,1,0:T(8,128)(2,1)} copy(bf16[4,16,32,1536]{3,1,2,0:T(8,128)(2,1)S(1)} %convert_bitcast_fusion.1) | data formatting | bytes 12582912 | tf_op jit(solution)/shard_map/convert_element_type | solution.py:33
  60.2 7.4 %copy.27 = bf16[1536,512,2]{0,2,1:T(2,128)(2,1)S(1)} copy(bf16[1536,512,2]{1,0,2:T(8,128)(2,1)} %fusion.7) | data formatting | bytes 6291456 | tf_op jit(solution)/shard_map/convert_element_type | solution.py:21
  70.3 10.0 %convert_bitcast_fusion.2 = bf16[1,1024,2048]{2,1,0:T(8,128)(2,1)S(1)} fusion(bf16[1536,1024]{0,1:T(8,128)(2,1)} %convert_element_type.69, bf16[2048,1536]{1,0:T(8,128)(2,1)} %bitcast.60), kind=kOutput, calls=%fused_computation.19 | convolution fusion | flops 6444548096 | bytes 13631488 | tf_op jit(solution)/shard_map/dot_general | solution.py:36
  80.3 24.6 %copy.67 = bf16[1,1024,2048]{2,0,1:T(2,128)(2,1)} copy(bf16[1,1024,2048]{2,1,0:T(8,128)(2,1)S(1)} %convert_bitcast_fusion.2) | data formatting | bytes 8388608 | tf_op jit(solution)/shard_map/reshape | solution.py:42
  105.5 27.4 %reduce.2 = bf16[1024,2048]{1,0:T(8,128)(2,1)} reduce(bf16[1024,1,2048]{2,1,0:T(2,128)(2,1)} %bitcast.56, bf16[]{:T(256)} %broadcast.88), dimensions={1}, to_apply=%bitcast.54.reduce_sub_computation | reduce | bytes 8388610
  132.9 11.4 %reshape.117 = bf16[16,2,65536]{2,1,0:T(2,128)(2,1)} reshape(bf16[1024,2048]{1,0:T(8,128)(2,1)} %reduce.2) | data formatting | bytes 8388608
  144.3 6.7 %all-to-all-start = ((bf16[16,2,65536]{2,1,0:T(2,128)(2,1)}), bf16[16,2,65536]{2,1,0:T(2,128)(2,1)}, u32[]{:S(2)}, u32[]{:S(2)}) async-start(bf16[16,2,65536]{2,1,0:T(2,128)(2,1)} %reshape.117), calls=%async_computation | async-start | bytes 8388608 | tf_op jit(solution)/shard_map/all_to_all | solution.py:50
  151.7 91.7 %all-to-all-done = bf16[16,2,65536]{2,1,0:T(2,128)(2,1)} async-done(((bf16[16,2,65536]{2,1,0:T(2,128)(2,1)}), bf16[16,2,65536]{2,1,0:T(2,128)(2,1)}, u32[]{:S(2)}, u32[]{:S(2)}) %all-to-all-start) | async-done | bytes 4194336 | tf_op jit(solution)/shard_map/all_to_all | solution.py:50
  243.4 12.7 %reshape.118 = bf16[1024,1,2048]{2,1,0:T(2,128)(2,1)} reshape(bf16[16,2,65536]{2,1,0:T(2,128)(2,1)} %all-to-all-done) | data formatting | bytes 8388608
  256.1 27.3 %bitcast_reduce_fusion = bf16[1024,2048]{1,0:T(8,128)(2,1)} fusion(bf16[1024,1,2048]{2,1,0:T(2,128)(2,1)} %reshape.118), kind=kLoop, calls=%fused_computation.36 | loop fusion | bytes 8388608 | tf_op jit(solution)/shard_map/all_to_all | solution.py:50
  283.4 19.5 %reshape.106 = bf16[16,32,2,64,32]{4,3,2,1,0:T(8,128)(2,1)} reshape(bf16[1024,2048]{1,0:T(8,128)(2,1)} %bitcast_reduce_fusion) | data formatting | bytes 8388608 | tf_op jit(solution)/shard_map/reshape | solution.py:51
  302.9 10.1 %fusion.2 = f32[32,2,64,256,1]{3,2,0,1,4:T(8,128)S(1)} fusion(bf16[16,32,2,64,32]{4,3,2,1,0:T(8,128)(2,1)} %reshape.106, bf16[32,16,32,256,1]{3,2,1,0,4:T(8,128)(2,1)} %bitcast.58), kind=kOutput, calls=%fused_computation.4 | convolution fusion | flops 1073741824 | bytes 16777216 | tf_op jit(solution)/shard_map/smrfa,msan->mrfn/dot_general | solution.py:53
  313.0 10.0 %convert_bitcast_fusion = bf16[16,32,2,64,32]{3,4,0,2,1:T(8,128)(2,1)} fusion(bf16[32,16,32,256,1]{3,2,1,4,0:T(8,128)(2,1)} %bitcast.59, f32[32,2,64,256,1]{3,2,0,1,4:T(8,128)S(1)} %fusion.2, f32[32,256]{1,0:T(8,128)S(1)} %fusion.21), kind=kOutput, calls=%fused_computation.9 | convolution fusion | flops 1077936128 | bytes 16809984 | tf_op jit(solution)/shard_map/mrfn,msan->smrfa/dot_general | solution.py:57
  323.0 15.9 %copy.33 = bf16[16,32,2,64,32]{4,3,2,1,0:T(8,128)(2,1)} copy(bf16[16,32,2,64,32]{3,4,0,2,1:T(8,128)(2,1)} %convert_bitcast_fusion) | data formatting | bytes 8388608 | tf_op jit(solution)/shard_map/convert_element_type | solution.py:60
  338.9 22.6 %reshape.108 = bf16[16,64,2048]{2,1,0:T(8,128)(2,1)} reshape(bf16[16,32,2,64,32]{4,3,2,1,0:T(8,128)(2,1)} %copy.33) | data formatting | bytes 8388608 | tf_op jit(solution)/shard_map/reshape | solution.py:60
  361.5 97.3 %all_to_all.8 = bf16[16,64,2048]{2,1,0:T(8,128)(2,1)} all-to-all(bf16[16,64,2048]{2,1,0:T(8,128)(2,1)} %reshape.108), channel_id=1, replica_groups=mesh['space'=16,'mem'=2] {'space'}, dimensions={0} | all-to-all | bytes 8388608 | tf_op jit(solution)/shard_map/all_to_all | solution.py:61
  458.8 6.6 %copy.34 = bf16[1024,2048]{0,1:T(8,128)(2,1)} copy(bf16[1024,2048]{1,0:T(8,128)(2,1)} %bitcast.57) | data formatting | bytes 8388608 | tf_op jit(solution)/shard_map/reshape | solution.py:63
  465.3 9.5 %fusion.9 = f32[4,16,32,1536]{3,1,2,0:T(8,128)S(1)} fusion(bf16[4,16,32,1024]{3,2,1,0:T(8,128)(2,1)} %bitcast.61, bf16[1536,1024]{0,1:T(8,128)(2,1)S(1)} %copy-done.2), kind=kOutput, calls=%fused_computation.17 | convolution fusion | flops 6442450944 | bytes 19922944 | tf_op jit(solution)/shard_map/dot_general | solution.py:62
  474.9 31.1 %fusion.1 = bf16[32,32,1536]{2,0,1:T(8,128)(2,1)} fusion(f32[4,16,32,1536]{3,1,2,0:T(8,128)S(1)} %fusion.9, bf16[4,32,32,1536]{3,2,1,0:T(8,128)(2,1)} %param.6, f32[16,32]{1,0:T(8,128)S(1)} %copy-done), kind=kOutput, calls=%fused_computation.3 | convolution fusion | flops 1225261056 | bytes 28313600 | tf_op jit(solution)/shard_map/jl,kjac->klac/dot_general | solution.py:69
  506.0 84.7 %all-reduce.2.cloned.1.call-done = bf16[32,32,1536]{2,0,1:T(8,128)(2,1)} async-done(((bf16[32,32,1536]{2,0,1:T(8,128)(2,1)}), bf16[32,32,1536]{2,0,1:T(8,128)(2,1)}) %all-reduce.2.cloned.1.call-update) | async-done | bytes 3145744 | tf_op jit(solution)/shard_map/psum | solution.py:71
  590.7 2.7 multiply_convert_fusion
  593.4 3.4 copy.37
  (18 shorter events, 7.7 us)
Async XLA Ops:
  6.5 25.5 %copy-start = (f32[16,32]{1,0:T(8,128)S(1)}, f32[16,32]{1,0:T(8,128)}, u32[]{:S(2)}) copy-start(f32[16,32]{1,0:T(8,128)} %param.8) | copy-start | bytes 6148
  6.5 23.7 %copy-start.3 = (bf16[32,32,1536]{2,1,0:T(8,128)(2,1)S(1)}, bf16[32,32,1536]{2,1,0:T(8,128)(2,1)}, u32[]{:S(2)}) copy-start(bf16[32,32,1536]{2,1,0:T(8,128)(2,1)} %param.7) | copy-start | bytes 9437188
  6.5 25.5 %copy-start.1 = (bf16[4,32,32,1536]{3,2,1,0:T(8,128)(2,1)S(1)}, bf16[4,32,32,1536]{3,2,1,0:T(8,128)(2,1)}, u32[]{:S(2)}) copy-start(bf16[4,32,32,1536]{3,2,1,0:T(8,128)(2,1)} %param.6) | copy-start | bytes 37748740
  144.3 7.4 %copy-start.4 = (f32[32,256]{1,0:T(8,128)S(1)}, f32[32,256]{1,0:T(8,128)}, u32[]{:S(2)}) copy-start(f32[32,256]{1,0:T(8,128)} %param.10) | copy-start | bytes 98308
  144.3 99.1 %all-to-all-start = ((bf16[16,2,65536]{2,1,0:T(2,128)(2,1)}), bf16[16,2,65536]{2,1,0:T(2,128)(2,1)}, u32[]{:S(2)}, u32[]{:S(2)}) async-start(bf16[16,2,65536]{2,1,0:T(2,128)(2,1)} %reshape.117), calls=%async_computation | async-start | bytes 8388608 | tf_op jit(solution)/shard_map/all_to_all | solution.py:50
  150.9 439.8 %all-reduce.2.cloned.1.call-start = ((), (), s32[]{:S(2)}) async-start(), calls=%async_computation.2 | async-start | bytes 6291456 | tf_op jit(solution)/shard_map/psum | solution.py:71
  458.8 6.6 %copy-start.2 = (bf16[1536,1024]{0,1:T(8,128)(2,1)S(1)}, bf16[1536,1024]{0,1:T(8,128)(2,1)}, u32[]{:S(2)}) copy-start(bf16[1536,1024]{0,1:T(8,128)(2,1)} %convert_element_type.69) | copy-start | bytes 9437188
Sparse Core Ops, SparseCore 0:
  506.1 84.5 all-reduce.1
where the time goes:
time: 612 us; the launch traced here: 604 us
  waiting for transfers between devices  176 us (29%)
  local copies, waits for them, and re-layouts  163 us (27%)
  blocking collectives  97.3 us (16%)
  matrix products  90.2 us (15%)
  other arithmetic  56.3 us (9%)
  between operations  14.4 us (2%)
  starting transfers between devices  6.69 us (1%)
    all_to_all x1, blocking collectives, on_device(): lax.all_to_all(synthesis, 'space', split_axis=0, concat_axis=1, tiled=True)  97.3 us
    all_to_all x1, waiting for transfers between devices, on_device(): lax.all_to_all(zonal_parts, 'space', split_axis=1, concat_axis=0, tiled=T...  91.7 us
    psum x1, waiting for transfers between devices, on_device(): lax.psum(partial_value.astype(jnp.bfloat16), 'mem').astype(jnp.float32)  84.7 us
    dot_general x1, matrix products, on_device(): lifted = jnp.einsum('jl,kjac->klac', modes, spread, precision=highest)  31.1 us
    unnamed x1, other arithmetic  27.4 us
    all_to_all x1, local copies, waits for them, and re-layouts, on_device(): lax.all_to_all(zonal_parts, 'space', split_axis=1, concat_axis=0, tiled=T...  27.3 us
    reshape x1, local copies, waits for them, and re-layouts, on_device(): zonal_parts = zonal_parts.astype(jnp.bfloat16).reshape(1, 2 * M, columns)  24.6 us
    unnamed x13, local copies, waits for them, and re-layouts  24.6 us
  transfers between devices with their start and end apart: 2, of which 2 were waited for; matrix products, arithmetic and copies ran while one was open for 0% of the time, Pallas kernels for 0%

commit v1 on v0

--- a/solution.py
+++ b/solution.py
@@ -3,6 +3,8 @@
 import jax
 import jax.numpy as jnp
 from jax import lax
+from jax.experimental import pallas as pl
+from jax.experimental.pallas import tpu as pltpu
 from jax.sharding import PartitionSpec as P
 
 NMODE = 16
@@ -21,7 +23,7 @@
     return stacked.reshape(length, 2 * wave_count).astype(jnp.bfloat16)
 
 
-def on_device(ensemble, vector, modes, legendre, spectrum, truncation):
+def plain_path(ensemble, vector, modes, legendre, spectrum, truncation):
     members = ensemble.shape[0]
     lat_rows = ensemble.shape[2]
     own_waves = legendre.shape[0]
@@ -72,6 +74,320 @@
     return (summed / (total_members - 1)).astype(jnp.bfloat16)
 
 
+F32 = jnp.float32
+BF16 = jnp.bfloat16
+TILE = 16
+LANES = 128
+BIG = 63 * 1024 * 1024
+
+
+def nt(a, b):
+    return lax.dot_general(a, b, (((1,), (1,)), ((), ())), preferred_element_type=F32)
+
+
+def nn(a, b):
+    return lax.dot_general(a, b, (((1,), (0,)), ((), ())), preferred_element_type=F32)
+
+
+def fourier_factors():
+    row = jnp.arange(2 * M, dtype=jnp.int32)[:, None]
+    lane = jnp.arange(LANES, dtype=jnp.int32)[None, :]
+    wave, part = row // 2, row % 2
+    step = 2.0 * math.pi / NLON
+    high = ((wave * LANES * lane + part * (NLON // 4)) % NLON).astype(F32) * step
+    low = (wave * lane % NLON).astype(F32) * step
+    amplitude = math.sqrt(2.0 / NLON)
+    return jnp.stack([jnp.cos(high) * amplitude, jnp.sin(high) * amplitude, jnp.cos(low), jnp.sin(low)])
+
+
+def build_table(factors_ref, table_ref):
+    rows = 128
+
+    @pl.loop(0, 2 * M // rows)
+    def _(i):
+        own = pl.ds(pl.multiple_of(i * rows, rows), rows)
+        low_cos, low_sin = factors_ref[2, own, :], factors_ref[3, own, :]
+        for high in range(NLON // LANES):
+            high_cos = factors_ref[0, own, high : high + 1]
+            high_sin = factors_ref[1, own, high : high + 1]
+            value = high_cos * low_cos - high_sin * low_sin
+            table_ref[own, high * LANES : (high + 1) * LANES] = value.astype(BF16)
+
+
+def greet(axis, count):
+    me = lax.axis_index(axis)
+    barrier = pltpu.get_barrier_semaphore()
+
+    @pl.loop(1, count)
+    def _(i):
+        pl.semaphore_signal(barrier, inc=1, device_id={axis: lax.rem(me + i, count)}, device_id_type=pl.DeviceIdType.MESH)
+
+    pl.semaphore_wait(barrier, count - 1)
+
+
+def send(axis, src, dst, send_sem, recv_sem, target):
+    return pltpu.make_async_remote_copy(
+        src_ref=src,
+        dst_ref=dst,
+        send_sem=send_sem,
+        recv_sem=recv_sem,
+        device_id={axis: target},
+        device_id_type=pl.DeviceIdType.MESH,
+    )
+
+
+def forward_kernel(sources, ens_hbm, vec_hbm, weight_ref, factors_ref, out_ref,
+                   ens, vec, table, fields, turn, packed, load_sem, own_sem, send_sem, recv_sem):
+    me = lax.axis_index("space")
+    members = ens.shape[0]
+    groups = ens.shape[2] // TILE
+    share = 2 * M // sources
+    width = 512
+    loads = [pltpu.make_async_copy(vec_hbm, vec, load_sem.at[members])]
+    loads += [pltpu.make_async_copy(ens_hbm.at[k], ens.at[k], load_sem.at[k]) for k in range(members)]
+    for load in loads:
+        load.start()
+    build_table(factors_ref, table)
+    greet("space", sources)
+    loads[0].wait()
+    levels = ens.shape[1]
+    for k in range(members):
+        loads[k + 1].wait()
+
+        @pl.loop(0, groups * (NLON // width))
+        def _(i):
+            g, c = i // (NLON // width), lax.rem(i, NLON // width)
+            rows = pl.ds(pl.multiple_of(g * TILE, TILE), TILE)
+            columns = pl.ds(pl.multiple_of(c * width, width), width)
+            product = ens[k, :, rows, columns] * vec[:, rows, columns]
+            result = nn(weight_ref[...], product.reshape(levels * TILE, width))
+            fields[:, g, k, :, columns] = result.astype(BF16).reshape(TILE, NMODE, width)
+
+    per_block = 4
+    lat_width = groups * members * NMODE
+
+    @pl.loop(0, sources // per_block)
+    def _(block):
+        targets = [lax.rem(me + block * per_block + i + 1, sources) for i in range(per_block)]
+        lhs = jnp.concatenate([table[pl.ds(pl.multiple_of(d * share, share), share), :] for d in targets], axis=0)
+        for pair in range(TILE // 2):
+            rhs = fields[2 * pair : 2 * pair + 2].reshape(2 * lat_width, NLON)
+            result = nt(lhs, rhs)
+            turn[:, 2 * pair, :] = result[:, :LANES]
+            turn[:, 2 * pair + 1, :] = result[:, LANES:]
+        for i in range(per_block):
+            slot = block * per_block + i
+            packed[slot] = turn[i * share : (i + 1) * share].astype(BF16)
+        for i in range(per_block):
+            slot = block * per_block + i
+
+            @pl.when(slot < sources - 1)
+            def _():
+                send("space", packed.at[slot], out_ref.at[me], send_sem.at[slot], recv_sem.at[me], targets[i]).start()
+
+    own = pltpu.make_async_copy(packed.at[sources - 1], out_ref.at[me], own_sem.at[0])
+    own.start()
+
+    @pl.loop(0, sources - 1)
+    def _(slot):
+        other = lax.rem(me + slot + 1, sources)
+        send("space", packed.at[slot], out_ref.at[other], send_sem.at[slot], recv_sem.at[other], other).wait()
+
+    own.wait()
+
+
+def spectral_kernel(sources, arrived, legendre, factor, out_ref,
+                    packed, own_sem, send_sem, recv_sem):
+    me = lax.axis_index("space")
+    own_waves = legendre.shape[0]
+    lat_rows = 2 * TILE
+    greet("space", sources)
+    half = LANES // 2
+
+    @pl.loop(0, own_waves)
+    def _(m):
+        table = legendre[m].reshape(sources, 2, TILE, NDEG)
+        halves = [table[:, h].reshape(sources * TILE, NDEG) for h in range(2)]
+        stacked = [arrived[:, 2 * m + r].reshape(sources * TILE, LANES).T for r in range(2)]
+        harmonic = 0.0
+        for h in range(2):
+            lhs = jnp.concatenate([z[h * half : (h + 1) * half] for z in stacked], axis=0)
+            harmonic = harmonic + nn(lhs, halves[h])
+        weighted = (harmonic * factor[pl.ds(m, 1), :]).astype(BF16)
+        zero = jnp.zeros((half, NDEG), BF16)
+        low = jnp.concatenate([weighted[:half], zero, weighted[half:], zero], axis=0)
+        high = jnp.concatenate([zero, weighted[:half], zero, weighted[half:]], axis=0)
+        synthesis = (nt(halves[0], low) + nt(halves[1], high)).astype(BF16)
+        for r in range(2):
+            block = synthesis[:, r * LANES : (r + 1) * LANES]
+            packed[:, 2 * m + r] = block.reshape(sources, TILE, LANES)
+
+    @pl.loop(1, sources)
+    def _(i):
+        other = lax.rem(me + i, sources)
+        send("space", packed.at[other], out_ref.at[me], send_sem.at[i], recv_sem.at[me], other).start()
+
+    own = pltpu.make_async_copy(packed.at[me], out_ref.at[me], own_sem.at[0])
+    own.start()
+
+    @pl.loop(1, sources)
+    def _(i):
+        other = lax.rem(me + i, sources)
+        send("space", packed.at[other], out_ref.at[other], send_sem.at[i], recv_sem.at[other], other).wait()
+
+    own.wait()
+
+
+def inverse_kernel(returned, ens_hbm, lift_ref, factors_ref, out_ref,
+                   ens, table, turn, fields, mine, theirs, load_sem, send_sem, recv_sem):
+    me = lax.axis_index("mem")
+    other = 1 - me
+    members, levels, lat_rows = ens.shape[:3]
+    groups = lat_rows // TILE
+    width = 512
+    pieces = NLON // width
+    load = pltpu.make_async_copy(ens_hbm, ens, load_sem.at[0])
+    load.start()
+    build_table(factors_ref, table)
+    greet("mem", 2)
+    sources, share = returned.shape[:2]
+
+    @pl.loop(0, sources)
+    def _(s):
+        turn[pl.ds(pl.multiple_of(s * share, share), share)] = returned[s].astype(F32)
+
+    for pair in range(TILE // 2):
+        lhs = jnp.concatenate([turn[:, 2 * pair + i, :].astype(BF16).T for i in range(2)], axis=0)
+
+        @pl.loop(0, pieces)
+        def _(c):
+            columns = pl.ds(pl.multiple_of(c * width, width), width)
+            result = nn(lhs, table[:, columns]).astype(BF16).reshape(2, groups, members, NMODE, width)
+            for i in range(2):
+                fields[:, :, 2 * pair + i, :, columns] = result[i]
+
+    load.wait()
+
+    @pl.loop(0, groups * pieces)
+    def _(i):
+        g, c = i // pieces, lax.rem(i, pieces)
+        rows = pl.ds(pl.multiple_of(g * TILE, TILE), TILE)
+        columns = pl.ds(pl.multiple_of(c * width, width), width)
+        total = 0.0
+        for k in range(members):
+            lifted = nn(lift_ref[...], fields[g, k, :, :, columns].reshape(TILE * NMODE, width))
+            anomaly = ens[k, :, rows, columns].reshape(levels * TILE, width)
+            total = total + lifted * anomaly.astype(F32)
+        mine[i] = total.astype(BF16)
+        send("mem", mine.at[i], theirs.at[i], send_sem.at[i], recv_sem.at[i], other).start()
+
+    scale = 1.0 / (2 * members - 1)
+
+    @pl.loop(0, groups * pieces)
+    def _(i):
+        g, c = i // pieces, lax.rem(i, pieces)
+        rows = pl.ds(pl.multiple_of(g * TILE, TILE), TILE)
+        columns = pl.ds(pl.multiple_of(c * width, width), width)
+        send("mem", mine.at[i], theirs.at[i], send_sem.at[i], recv_sem.at[i], other).wait()
+        summed = (mine[i].astype(F32) + theirs[i].astype(F32)) * scale
+        out_ref[:, rows, columns] = summed.astype(BF16).reshape(levels, TILE, width)
+
+
+def params(number):
+    return pltpu.CompilerParams(collective_id=number, has_side_effects=True, vmem_limit_bytes=BIG)
+
+
+def kernel_path(ensemble, vector, modes, legendre, spectrum, truncation):
+    members, levels, lat_rows, _ = ensemble.shape
+    own_waves = legendre.shape[0]
+    sources = lax.axis_size("space")
+    share = 2 * own_waves
+    factors = fourier_factors()
+    same = jnp.eye(TILE, dtype=F32)
+    weight = same[:, None, None, :] * modes[None, :, :, None]
+    weight = weight.reshape(TILE * NMODE, levels * TILE).astype(BF16)
+    lift = same[None, :, :, None] * modes.T[:, None, None, :]
+    lift = lift.reshape(levels * TILE, TILE * NMODE).astype(BF16)
+    wavenumber = (
+        lax.axis_index("space") * own_waves
+        + jnp.arange(own_waves, dtype=jnp.int32)[:, None]
+        + jnp.arange(NDEG, dtype=jnp.int32)[None, :]
+    )
+    factor = jnp.where(wavenumber <= truncation[0], spectrum, jnp.zeros_like(spectrum))
+    any_space = pl.BlockSpec(memory_space=pl.ANY)
+    vmem = pl.BlockSpec(memory_space=pltpu.VMEM)
+    exchanged = jax.ShapeDtypeStruct((sources, share, TILE, LANES), BF16)
+    groups = lat_rows // TILE
+    width = 512
+    pieces = groups * (NLON // width)
+    dma = pltpu.SemaphoreType.DMA
+    arrived = pl.pallas_call(
+        lambda *refs: forward_kernel(sources, *refs),
+        out_shape=exchanged,
+        in_specs=[any_space, any_space, vmem, vmem],
+        out_specs=any_space,
+        scratch_shapes=[
+            pltpu.VMEM(ensemble.shape, BF16),
+            pltpu.VMEM(vector.shape, BF16),
+            pltpu.VMEM((2 * M, NLON), BF16),
+            pltpu.VMEM((TILE, groups, members, NMODE, NLON), BF16),
+            pltpu.VMEM((4 * share, TILE, LANES), F32),
+            pltpu.VMEM((sources, share, TILE, LANES), BF16),
+            dma((members + 1,)),
+            dma((1,)),
+            dma((sources,)),
+            dma((sources,)),
+        ],
+        compiler_params=params(0),
+        name="forward",
+    )(ensemble, vector, weight, factors)
+    returned = pl.pallas_call(
+        lambda *refs: spectral_kernel(sources, *refs),
+        out_shape=exchanged,
+        in_specs=[vmem, vmem, vmem],
+        out_specs=any_space,
+        scratch_shapes=[
+            pltpu.VMEM((sources, share, TILE, LANES), BF16),
+            dma((1,)),
+            dma((sources,)),
+            dma((sources,)),
+        ],
+        compiler_params=params(1),
+        name="spectral",
+    )(arrived, legendre, factor)
+    return pl.pallas_call(
+        inverse_kernel,
+        out_shape=jax.ShapeDtypeStruct(vector.shape, BF16),
+        in_specs=[vmem, any_space, vmem, vmem],
+        out_specs=vmem,
+        scratch_shapes=[
+            pltpu.VMEM(ensemble.shape, BF16),
+            pltpu.VMEM((2 * M, NLON), BF16),
+            pltpu.VMEM((2 * M, TILE, LANES), F32),
+            pltpu.VMEM((groups, members, TILE, NMODE, NLON), BF16),
+            pltpu.VMEM((pieces, levels * TILE, width), BF16),
+            pltpu.VMEM((pieces, levels * TILE, width), BF16),
+            dma((1,)),
+            dma((pieces,)),
+            dma((pieces,)),
+        ],
+        compiler_params=params(2),
+        name="inverse",
+    )(returned, ensemble, lift, factors)
+
+
+def on_device(ensemble, vector, modes, legendre, spectrum, truncation):
+    fits = (
+        lax.axis_size("mem") == 2
+        and lax.axis_size("space") % 4 == 0
+        and ensemble.shape[2] == 2 * TILE
+        and 2 * ensemble.shape[0] * NMODE == LANES
+        and modes.shape[1] == 32
+    )
+    path = kernel_path if fits else plain_path
+    return path(ensemble, vector, modes, legendre, spectrum, truncation)
+
+
 def solution(mesh):
     placed = (
         P("mem", None, "space", None),

time: 612 us -> 345 us (0.56); the launches traced: 604 us -> 345 us
  Pallas kernels: 0 us -> 325 us
  waiting for transfers between devices: 176 us -> 0 us
  local copies, waits for them, and re-layouts: 163 us -> 11.1 us
  blocking collectives: 97.3 us -> 0 us
  matrix products: 90.2 us -> 0 us
  other arithmetic: 56.3 us -> 7.66 us
  between operations: 14.4 us -> 0.73 us
  starting transfers between devices: 6.69 us -> 0 us
    pallas_call x0 -> x3, Pallas kernels: none -> 325 us  [the longest x1 115 us: kernel_path(): pl.pallas_call(lambda *refs: spectral_kernel(sources, *refs), out_shape=e...]
    all_to_all x1 -> x0, blocking collectives: 97.3 us -> none  [on_device(): lax.all_to_all(synthesis, 'space', split_axis=0, concat_axis=1, tiled=True)]
    all_to_all x1 -> x0, waiting for transfers between devices: 91.7 us -> none  [on_device(): lax.all_to_all(zonal_parts, 'space', split_axis=1, concat_axis=0, tiled=T...]
    dot_general x6 -> x0, matrix products: 90.2 us -> none  [the longest x1 31.1 us: on_device(): lifted = jnp.einsum('jl,kjac->klac', modes, spread, precision=highest)]
    psum x1 -> x0, waiting for transfers between devices: 84.7 us -> none  [on_device(): lax.psum(partial_value.astype(jnp.bfloat16), 'mem').astype(jnp.float32)]
    reshape x4 -> x0, local copies, waits for them, and re-layouts: 73.3 us -> none  [the longest x1 24.6 us: on_device(): zonal_parts = zonal_parts.astype(jnp.bfloat16).reshape(1, 2 * M, columns)]
    convert_element_type x6 -> x2, local copies, waits for them, and re-layouts: 37.4 us -> 7.1 us  [the longest x1 4.42 us: kernel_path(): weight = weight.reshape(TILE * NMODE, levels * TILE).astype(BF16)]
    unnamed x1 -> x0, other arithmetic: 27.4 us -> none
  transfers between devices with their start and end apart: 2 -> 0, of which waited for: 2 -> 0; matrix products, arithmetic and copies ran while one was open for 0% -> 0% of each run, Pallas kernels for 0% -> 0%
where the time goes in v1:
time: 345 us
  Pallas kernels  325 us (94%)
  local copies, waits for them, and re-layouts  11.1 us (3%)
  other arithmetic  7.66 us (2%)
    pallas_call x1, Pallas kernels, kernel_path(): pl.pallas_call(lambda *refs: spectral_kernel(sources, *refs), out_shape=e...  115 us
    pallas_call x1, Pallas kernels, kernel_path(): pl.pallas_call(lambda *refs: forward_kernel(sources, *refs), out_shape=ex...  112 us
    pallas_call x1, Pallas kernels, kernel_path(): pl.pallas_call(inverse_kernel, out_shape=jax.ShapeDtypeStruct(vector.shap...  98.6 us

profile of v1, /device:TPU:15, one launch (start us, length us, event | category | flops | bytes accessed | tf_op | source)
XLA Modules:
  0.0 344.7 jit_solution(403787279530613779)
XLA Ops:
  0.0 0.0 copy-start
  0.0 2.3 cosine_multiply_fusion
  2.3 2.2 fusion.7
  4.5 1.5 pad_maximum_fusion.refs_3_.factors_ref
  5.9 0.0 copy-done
  5.9 0.5 multiply_convert_fusion.1
  6.4 4.4 %convert_element_type.57.refs_2_ = bf16[256,512]{1,0:T(8,128)(2,1)} reshape(bf16[16,16,32,16]{3,2,1,0:T(8,128)(2,1)S(1)} %multiply_convert_fusion.1) | data formatting | bytes 524288 | tf_op jit(solution)/shard_map/convert_element_type | solution.py:308
  10.9 0.0 copy-start.1
  10.9 111.8 %forward.1.refs_0_ = bf16[16,64,16,128]{3,2,1,0:T(8,128)(2,1)} custom-call(bf16[4,32,32,1536]{3,2,1,0:T(8,128)(2,1)} %ens_hbm.1, bf16[32,32,1536]{2,1,0:T(8,128)(2,1)} %refs_1_.2, bf16[256,512]{1,0:T(8,128)(2,1)} %convert_element_type.57.refs_2_, f32[4,1024,128]{2,1,0:T(8,128)} %pad_maximum_fusion.refs_3_.factors_ref), custom_call_target="tpu_custom_call" | custom-call | tf_op jit(solution)/shard_map/forward/pallas_call | solution.py:324
  123.3 0.0 copy-done.1
  123.3 0.7 fusion.12.refs_2_
  124.0 114.9 %spectral.1.returned = bf16[16,64,16,128]{3,2,1,0:T(8,128)(2,1)} custom-call(bf16[16,64,16,128]{3,2,1,0:T(8,128)(2,1)} %forward.1.refs_0_, bf16[32,512,256]{2,1,0:T(8,128)(2,1)} %refs_1_.3, f32[32,256]{1,0:T(8,128)} %fusion.12.refs_2_), custom_call_target="tpu_custom_call" | custom-call | tf_op jit(solution)/shard_map/spectral/pallas_call | solution.py:344
  238.9 0.1 copy.8
  238.9 0.6 multiply_convert_fusion
  239.5 2.7 convert_element_type.61.lift_ref
  242.2 98.6 %inverse.1 = bf16[32,32,1536]{2,1,0:T(8,128)(2,1)} custom-call(bf16[16,64,16,128]{3,2,1,0:T(8,128)(2,1)} %spectral.1.returned, bf16[4,32,32,1536]{3,2,1,0:T(8,128)(2,1)} %ens_hbm.1, bf16[512,256]{1,0:T(8,128)(2,1)} %convert_element_type.61.lift_ref, f32[4,1024,128]{2,1,0:T(8,128)} %pad_maximum_fusion.refs_3_.factors_ref), custom_call_target="tpu_custom_call" | custom-call | tf_op jit(solution)/shard_map/inverse/pallas_call | solution.py:358
  340.8 3.9 %copy.11 = bf16[32,32,1536]{2,1,0:T(8,128)(2,1)} copy(bf16[32,32,1536]{2,1,0:T(8,128)(2,1)} %inverse.1) | data formatting | bytes 6291456
  (4 shorter events, 0.0 us)
Async XLA Ops:
  0.0 5.9 %copy-start = (f32[16,32]{1,0:T(8,128)S(1)}, f32[16,32]{1,0:T(8,128)}, u32[]{:S(2)}) copy-start(f32[16,32]{1,0:T(8,128)} %param.8) | copy-start | bytes 6148
  10.9 112.4 %copy-start.1 = (f32[32,256]{1,0:T(8,128)S(1)}, f32[32,256]{1,0:T(8,128)}, u32[]{:S(2)}) copy-start(f32[32,256]{1,0:T(8,128)} %param.10) | copy-start | bytes 98308

commit v2 on v0

--- a/solution.py
+++ b/solution.py
@@ -3,6 +3,8 @@
 import jax
 import jax.numpy as jnp
 from jax import lax
+from jax.experimental import pallas as pl
+from jax.experimental.pallas import tpu as pltpu
 from jax.sharding import PartitionSpec as P
 
 NMODE = 16
@@ -21,7 +23,7 @@
     return stacked.reshape(length, 2 * wave_count).astype(jnp.bfloat16)
 
 
-def on_device(ensemble, vector, modes, legendre, spectrum, truncation):
+def plain_path(ensemble, vector, modes, legendre, spectrum, truncation):
     members = ensemble.shape[0]
     lat_rows = ensemble.shape[2]
     own_waves = legendre.shape[0]
@@ -72,6 +74,350 @@
     return (summed / (total_members - 1)).astype(jnp.bfloat16)
 
 
+F32 = jnp.float32
+BF16 = jnp.bfloat16
+TILE = 16
+LANES = 128
+BIG = 63 * 1024 * 1024
+
+
+def nt(a, b):
+    return lax.dot_general(a, b, (((1,), (1,)), ((), ())), preferred_element_type=F32)
+
+
+def nn(a, b):
+    return lax.dot_general(a, b, (((1,), (0,)), ((), ())), preferred_element_type=F32)
+
+
+def cosine(phase):
+    phase = lax.rem(phase, NLON)
+    offset = (jnp.abs(phase - NLON // 2) - NLON // 4).astype(F32)
+    x = offset * (2.0 * math.pi / NLON)
+    square = x * x
+    value = 1.0
+    for n in range(6, 0, -1):
+        value = 1.0 - square * value * (1.0 / ((2 * n) * (2 * n + 1)))
+    return x * value
+
+
+def build_table(table_ref, waves_first):
+    rows = 128
+    quarter = NLON // 4
+    amplitude = math.sqrt(2.0 / NLON)
+
+    @pl.loop(0, 2 * M // rows)
+    def _(i):
+        start = pl.multiple_of(i * rows, rows)
+        row = start + lax.broadcasted_iota(jnp.int32, (rows, LANES), 0)
+        lane = lax.broadcasted_iota(jnp.int32, (rows, LANES), 1)
+        wave, part = (lax.rem(row, M), row // M) if waves_first else (row // 2, lax.rem(row, 2))
+        low_cos = cosine(wave * lane)
+        low_sin = cosine(wave * lane + 3 * quarter)
+        high = cosine(wave * LANES * lax.rem(lane, 64) + (part + 3 * (lane // 64)) * quarter) * amplitude
+        for c in range(NLON // LANES):
+            value = high[:, c : c + 1] * low_cos - high[:, 64 + c : 65 + c] * low_sin
+            table_ref[pl.ds(start, rows), c * LANES : (c + 1) * LANES] = value.astype(BF16)
+
+
+def greet(counts):
+    barrier = pltpu.get_barrier_semaphore()
+    for axis, count in counts:
+        me = lax.axis_index(axis)
+        for i in range(1, count):
+            target = lax.rem(me + i, count)
+            pl.semaphore_signal(barrier, inc=1, device_id={axis: target}, device_id_type=pl.DeviceIdType.MESH)
+    pl.semaphore_wait(barrier, sum(count - 1 for _, count in counts))
+
+
+def send(axis, src, dst, send_sem, recv_sem, target):
+    return pltpu.make_async_remote_copy(
+        src_ref=src,
+        dst_ref=dst,
+        send_sem=send_sem,
+        recv_sem=recv_sem,
+        device_id={axis: target},
+        device_id_type=pl.DeviceIdType.MESH,
+    )
+
+
+def spread_modes(modes_ref, levels, across):
+    tiled = jnp.concatenate([modes_ref[...]] * TILE, axis=0)
+    long, short = levels * TILE, TILE * NMODE
+    if across:
+        pick = (lax.broadcasted_iota(jnp.int32, (levels, long), 1) // TILE) == lax.broadcasted_iota(jnp.int32, (levels, long), 0)
+        value = nn(tiled, jnp.where(pick, 1.0, 0.0).astype(BF16))
+        shape, long_at = (short, long), 1
+    else:
+        pick = (lax.broadcasted_iota(jnp.int32, (long, levels), 0) // TILE) == lax.broadcasted_iota(jnp.int32, (long, levels), 1)
+        value = nt(jnp.where(pick, 1.0, 0.0).astype(BF16), tiled)
+        shape, long_at = (long, short), 0
+    agree = (lax.broadcasted_iota(jnp.int32, shape, long_at) % TILE) == (lax.broadcasted_iota(jnp.int32, shape, 1 - long_at) // NMODE)
+    return jnp.where(agree, value, 0.0).astype(BF16)
+
+
+ROW = 4
+STEPS = (2, 1, 3, 0)
+
+
+class Exchange:
+    def __init__(self, sources, sources_at, landing_at, own_sem, send_sem, recv_sem):
+        self.count = sources // ROW
+        self.me = lax.axis_index("space")
+        self.row, self.column = self.me // ROW, lax.rem(self.me, ROW)
+        self.sources_at, self.landing_at = sources_at, landing_at
+        self.own_sem, self.send_sem, self.recv_sem = own_sem, send_sem, recv_sem
+
+    def device(self, step, i):
+        return lax.rem(self.row + step + self.count, self.count) * ROW + lax.rem(self.column + i + ROW, ROW)
+
+    def piece(self, step, i, part, source):
+        at = step * ROW + i
+        return send("space", self.sources_at(step, i, part), self.landing_at(source, part),
+                    self.send_sem.at[part, at], self.recv_sem.at[part, at], self.device(step, i))
+
+    def own(self, part):
+        return pltpu.make_async_copy(self.sources_at(0, 0, part), self.landing_at(self.me, part), self.own_sem.at[part])
+
+    def start(self, step, part):
+        for i in range(ROW):
+            if step == 0 and i == 0:
+                self.own(part).start()
+            else:
+                self.piece(step, i, part, self.me).start()
+
+    def finish(self, part):
+        for step in STEPS:
+            for i in range(ROW):
+                if step == 0 and i == 0:
+                    self.own(part).wait()
+                else:
+                    self.piece(step, i, part, self.device(-step, -i)).wait()
+
+
+def forward_kernel(sources, ens_hbm, vec_hbm, modes_ref, out_ref,
+                   weight_ref, ens, vec, table, fields, turn, packed, load_sem, *sems):
+    me = lax.axis_index("space")
+    members = ens.shape[0]
+    groups = ens.shape[2] // TILE
+    share = 2 * M // sources
+    width = 512
+    loads = [pltpu.make_async_copy(vec_hbm, vec, load_sem.at[members])]
+    loads += [pltpu.make_async_copy(ens_hbm.at[k], ens.at[k], load_sem.at[k]) for k in range(members)]
+    for load in loads:
+        load.start()
+    levels = ens.shape[1]
+    weight_ref[...] = spread_modes(modes_ref, levels, True)
+    build_table(table, False)
+    greet((("space", sources),))
+    loads[0].wait()
+    for k in range(members):
+        loads[k + 1].wait()
+
+        @pl.loop(0, groups * (NLON // width))
+        def _(i):
+            g, c = i // (NLON // width), lax.rem(i, NLON // width)
+            rows = pl.ds(pl.multiple_of(g * TILE, TILE), TILE)
+            columns = pl.ds(pl.multiple_of(c * width, width), width)
+            product = ens[k, :, rows, columns] * vec[:, rows, columns]
+            result = nn(weight_ref[...], product.reshape(levels * TILE, width))
+            result = result.astype(BF16).reshape(2, TILE // 2, NMODE, width)
+            for h in range(2):
+                fields[pl.ds(g * (TILE // 2), TILE // 2), h, k, :, columns] = result[h]
+
+    lat_width = groups * members * NMODE
+    trade = Exchange(sources, lambda step, i, part: packed.at[step * ROW + i], lambda source, part: out_ref.at[source], *sems)
+    for step in STEPS:
+        lhs = jnp.concatenate(
+            [table[pl.ds(pl.multiple_of(trade.device(step, i) * share, share), share), :] for i in range(ROW)], axis=0
+        )
+        for pair in range(TILE // 2):
+            rhs = fields[2 * pair : 2 * pair + 2].reshape(2 * lat_width, NLON)
+            result = nt(lhs, rhs)
+            turn[:, 2 * pair, :] = result[:, :LANES]
+            turn[:, 2 * pair + 1, :] = result[:, LANES:]
+        for i in range(ROW):
+            packed[step * ROW + i] = turn[i * share : (i + 1) * share].astype(BF16)
+        trade.start(step, 0)
+    trade.finish(0)
+
+
+def inverse_kernel(sources, arrived, legendre, factor, ens_hbm, modes_ref, out_ref,
+                   landing, packed, lift_ref, ens, table, turn, turned, fields, mine, theirs,
+                   load_sem, mem_send, mem_recv, *sems):
+    own_waves = legendre.shape[0]
+    members, levels, lat_rows = ens.shape[:3]
+    groups = lat_rows // TILE
+    eight = TILE // 2
+    half = LANES // 2
+    middle = own_waves // 2
+    width = mine.shape[2]
+    pieces = NLON // width
+    load = pltpu.make_async_copy(ens_hbm, ens, load_sem.at[0])
+    load.start()
+
+    trade = Exchange(
+        sources,
+        lambda step, i, part: packed.at[trade.device(step, i), part // 2, pl.ds(part % 2 * middle, middle)],
+        lambda source, part: landing.at[source, part // 2, pl.ds(part % 2 * middle, middle)],
+        *sems,
+    )
+    other = 1 - lax.axis_index("mem")
+    greet((("space", sources), ("mem", 2)))
+
+    def wave(m):
+        rows = legendre[m].astype(F32).reshape(sources * groups, 2, eight, NDEG)
+        halves = [rows[:, h].reshape(sources * TILE, NDEG).astype(BF16) for h in range(2)]
+        stacked = [arrived[:, 2 * m + r].reshape(sources * TILE, LANES).T for r in range(2)]
+        harmonic = 0.0
+        for h in range(2):
+            lhs = jnp.concatenate([z[h * half : (h + 1) * half] for z in stacked], axis=0)
+            harmonic = harmonic + nn(lhs, halves[h])
+        weighted = (harmonic * factor[pl.ds(m, 1), :]).astype(BF16)
+        zero = jnp.zeros((half, NDEG), BF16)
+        low = jnp.concatenate([weighted[:half], zero, weighted[half:], zero], axis=0)
+        high = jnp.concatenate([zero, weighted[:half], zero, weighted[half:]], axis=0)
+        synthesis = nt(halves[0], low) + nt(halves[1], high)
+        parts = [synthesis[:, r * LANES : (r + 1) * LANES].reshape(sources, groups, eight, LANES) for r in range(2)]
+        packed[:, :, m] = jnp.concatenate(parts, axis=2).astype(BF16)
+
+    pl.loop(0, middle)(wave)
+    for step in STEPS:
+        trade.start(step, 0)
+    pl.loop(middle, own_waves)(wave)
+    for part in (1, 2, 3):
+        for step in STEPS:
+            trade.start(step, part)
+    lift_ref[...] = spread_modes(modes_ref, levels, False)
+    build_table(table, True)
+    load.wait()
+    for g in range(groups):
+        trade.finish(2 * g)
+        trade.finish(2 * g + 1)
+
+        @pl.loop(0, sources)
+        def _(source):
+            turn[pl.ds(pl.multiple_of(source * own_waves, own_waves), own_waves)] = landing[source, g].astype(F32)
+
+        for t in range(eight):
+            column = jnp.concatenate([turn[:, r * eight + t, :] for r in range(2)], axis=0)
+            turned[t] = column.astype(BF16).T
+
+        @pl.loop(0, pieces)
+        def _(c):
+            columns = pl.ds(pl.multiple_of(c * width, width), width)
+            for quad in range(eight // 4):
+                lhs = turned[4 * quad : 4 * quad + 4].reshape(4 * LANES, 2 * M)
+                result = nn(lhs, table[:, columns]).astype(BF16).reshape(4, 2, members, NMODE, width)
+                for i in range(4):
+                    for h in range(2):
+                        fields[:, h * eight + 4 * quad + i] = result[i, h]
+            total = 0.0
+            for k in range(members):
+                lifted = nn(lift_ref[...], fields[k].reshape(TILE * NMODE, width))
+                anomaly = ens[k, :, g * TILE : (g + 1) * TILE, columns].reshape(levels * TILE, width)
+                total = total + lifted * anomaly.astype(F32)
+            at = g * pieces + c
+            mine[at] = total.astype(BF16)
+            send("mem", mine.at[at], theirs.at[at], mem_send.at[at], mem_recv.at[at], other).start()
+
+    scale = 1.0 / (2 * members - 1)
+    for g in range(groups):
+
+        @pl.loop(0, pieces)
+        def _(c):
+            at = g * pieces + c
+            columns = pl.ds(pl.multiple_of(c * width, width), width)
+            send("mem", mine.at[at], theirs.at[at], mem_send.at[at], mem_recv.at[at], other).wait()
+            summed = (mine[at].astype(F32) + theirs[at].astype(F32)) * scale
+            out_ref[:, g * TILE : (g + 1) * TILE, columns] = summed.astype(BF16).reshape(levels, TILE, width)
+
+
+def params(number):
+    return pltpu.CompilerParams(collective_id=number, has_side_effects=True, vmem_limit_bytes=BIG)
+
+
+def kernel_path(ensemble, vector, modes, legendre, spectrum, truncation):
+    members, levels, lat_rows, _ = ensemble.shape
+    own_waves = legendre.shape[0]
+    sources = lax.axis_size("space")
+    share = 2 * own_waves
+    narrow = modes.astype(BF16)
+    wavenumber = (
+        lax.axis_index("space") * own_waves
+        + jnp.arange(own_waves, dtype=jnp.int32)[:, None]
+        + jnp.arange(NDEG, dtype=jnp.int32)[None, :]
+    )
+    factor = jnp.where(wavenumber <= truncation[0], spectrum, jnp.zeros_like(spectrum))
+    any_space = pl.BlockSpec(memory_space=pl.ANY)
+    vmem = pl.BlockSpec(memory_space=pltpu.VMEM)
+    exchanged = jax.ShapeDtypeStruct((sources, share, TILE, LANES), BF16)
+    groups = lat_rows // TILE
+    width = 256
+    pieces = groups * (NLON // width)
+    dma = pltpu.SemaphoreType.DMA
+    arrived = pl.pallas_call(
+        lambda *refs: forward_kernel(sources, *refs),
+        out_shape=exchanged,
+        in_specs=[any_space, any_space, vmem],
+        out_specs=any_space,
+        scratch_shapes=[
+            pltpu.VMEM((TILE * NMODE, levels * TILE), BF16),
+            pltpu.VMEM(ensemble.shape, BF16),
+            pltpu.VMEM(vector.shape, BF16),
+            pltpu.VMEM((2 * M, NLON), BF16),
+            pltpu.VMEM((TILE, 2, members, NMODE, NLON), BF16),
+            pltpu.VMEM((4 * share, TILE, LANES), F32),
+            pltpu.VMEM((sources, share, TILE, LANES), BF16),
+            dma((members + 1,)),
+            dma((1,)),
+            dma((1, sources)),
+            dma((1, sources)),
+        ],
+        compiler_params=params(0),
+        name="forward",
+    )(ensemble, vector, narrow)
+    traded = pltpu.VMEM((sources, groups, own_waves, TILE, LANES), BF16)
+    parts = 2 * groups
+    return pl.pallas_call(
+        lambda *refs: inverse_kernel(sources, *refs),
+        out_shape=jax.ShapeDtypeStruct(vector.shape, BF16),
+        in_specs=[vmem, vmem, vmem, any_space, vmem],
+        out_specs=vmem,
+        scratch_shapes=[
+            traded,
+            traded,
+            pltpu.VMEM((levels * TILE, TILE * NMODE), BF16),
+            pltpu.VMEM(ensemble.shape, BF16),
+            pltpu.VMEM((2 * M, NLON), BF16),
+            pltpu.VMEM((M, TILE, LANES), F32),
+            pltpu.VMEM((TILE // 2, LANES, 2 * M), BF16),
+            pltpu.VMEM((members, TILE, NMODE, width), BF16),
+            pltpu.VMEM((pieces, levels * TILE, width), BF16),
+            pltpu.VMEM((pieces, levels * TILE, width), BF16),
+            dma((1,)),
+            dma((pieces,)),
+            dma((pieces,)),
+            dma((parts,)),
+            dma((parts, sources)),
+            dma((parts, sources)),
+        ],
+        compiler_params=params(1),
+        name="inverse",
+    )(arrived, legendre, factor, ensemble, narrow)
+
+
+def on_device(ensemble, vector, modes, legendre, spectrum, truncation):
+    fits = (
+        lax.axis_size("mem") == 2
+        and lax.axis_size("space") == 4 * ROW
+        and ensemble.shape[2] == 2 * TILE
+        and 2 * ensemble.shape[0] * NMODE == LANES
+        and modes.shape[1] == 32
+    )
+    path = kernel_path if fits else plain_path
+    return path(ensemble, vector, modes, legendre, spectrum, truncation)
+
+
 def solution(mesh):
     placed = (
         P("mem", None, "space", None),

time: 612 us -> 280 us (0.46); the launches traced: 604 us -> 279 us
  Pallas kernels: 0 us -> 272 us
  waiting for transfers between devices: 176 us -> 0 us
  local copies, waits for them, and re-layouts: 163 us -> 3.88 us
  blocking collectives: 97.3 us -> 0 us
  matrix products: 90.2 us -> 0 us
  other arithmetic: 56.3 us -> 2.74 us
  between operations: 14.4 us -> 0.68 us
  starting transfers between devices: 6.69 us -> 0 us
    pallas_call x0 -> x2, Pallas kernels: none -> 272 us  [the longest x1 159 us: kernel_path(): pl.pallas_call(lambda *refs: inverse_kernel(sources, *refs), out_shape=ja...]
    all_to_all x1 -> x0, blocking collectives: 97.3 us -> none  [on_device(): lax.all_to_all(synthesis, 'space', split_axis=0, concat_axis=1, tiled=True)]
    all_to_all x1 -> x0, waiting for transfers between devices: 91.7 us -> none  [on_device(): lax.all_to_all(zonal_parts, 'space', split_axis=1, concat_axis=0, tiled=T...]
    dot_general x6 -> x0, matrix products: 90.2 us -> none  [the longest x1 31.1 us: on_device(): lifted = jnp.einsum('jl,kjac->klac', modes, spread, precision=highest)]
    psum x1 -> x0, waiting for transfers between devices: 84.7 us -> none  [on_device(): lax.psum(partial_value.astype(jnp.bfloat16), 'mem').astype(jnp.float32)]
    reshape x4 -> x0, local copies, waits for them, and re-layouts: 73.3 us -> none  [the longest x1 24.6 us: on_device(): zonal_parts = zonal_parts.astype(jnp.bfloat16).reshape(1, 2 * M, columns)]
    convert_element_type x6 -> x0, local copies, waits for them, and re-layouts: 37.4 us -> none  [the longest x1 15.9 us: on_device(): synthesis.astype(jnp.bfloat16).reshape(sources, 2 * own_waves, columns)]
    unnamed x1 -> x0, other arithmetic: 27.4 us -> none
  transfers between devices with their start and end apart: 2 -> 0, of which waited for: 2 -> 0; matrix products, arithmetic and copies ran while one was open for 0% -> 0% of each run, Pallas kernels for 0% -> 0%
where the time goes in v2:
time: 280 us; the launch traced here: 279 us
  Pallas kernels  272 us (97%)
  local copies, waits for them, and re-layouts  3.88 us (1%)
    pallas_call x1, Pallas kernels, kernel_path(): pl.pallas_call(lambda *refs: inverse_kernel(sources, *refs), out_shape=ja...  159 us
    pallas_call x1, Pallas kernels, kernel_path(): pl.pallas_call(lambda *refs: forward_kernel(sources, *refs), out_shape=ex...  112 us

profile of v2, /device:TPU:15, one launch (start us, length us, event | category | flops | bytes accessed | tf_op | source)
XLA Modules:
  0.0 278.9 jit_solution(6022479950019860469)
XLA Ops:
  0.7 1.3 convert_element_type.3.refs_2_.refs_4_
  2.0 1.4 fusion.refs_2_
  3.4 112.3 %forward.1.refs_0_ = bf16[16,64,16,128]{3,2,1,0:T(8,128)(2,1)} custom-call(bf16[4,32,32,1536]{3,2,1,0:T(8,128)(2,1)} %refs_3_.1, bf16[32,32,1536]{2,1,0:T(8,128)(2,1)} %refs_1_.2, bf16[16,32]{1,0:T(8,128)(2,1)} %convert_element_type.3.refs_2_.refs_4_), custom_call_target="tpu_custom_call" | custom-call | tf_op jit(solution)/shard_map/forward/pallas_call | solution.py:358
  115.8 159.3 %inverse.1 = bf16[32,32,1536]{2,1,0:T(8,128)(2,1)} custom-call(bf16[16,64,16,128]{3,2,1,0:T(8,128)(2,1)} %forward.1.refs_0_, bf16[32,512,256]{2,1,0:T(8,128)(2,1)} %refs_1_.3, f32[32,256]{1,0:T(8,128)} %fusion.refs_2_, bf16[4,32,32,1536]{3,2,1,0:T(8,128)(2,1)} %refs_3_.1, bf16[16,32]{1,0:T(8,128)(2,1)} %convert_element_type.3.refs_2_.refs_4_), custom_call_target="tpu_custom_call" | custom-call | tf_op jit(solution)/shard_map/inverse/pallas_call | solution.py:381
  275.1 3.9 %copy.9 = bf16[32,32,1536]{2,1,0:T(8,128)(2,1)} copy(bf16[32,32,1536]{2,1,0:T(8,128)(2,1)} %inverse.1) | data formatting | bytes 6291456
  (1 shorter events, 0.0 us)

commit v3 on v2

--- a/solution.py
+++ b/solution.py
@@ -141,7 +141,7 @@
 
 
 def spread_modes(modes_ref, levels, across):
-    tiled = jnp.concatenate([modes_ref[...]] * TILE, axis=0)
+    tiled = jnp.concatenate([modes_ref[...].astype(BF16)] * TILE, axis=0)
     long, short = levels * TILE, TILE * NMODE
     if across:
         pick = (lax.broadcasted_iota(jnp.int32, (levels, long), 1) // TILE) == lax.broadcasted_iota(jnp.int32, (levels, long), 0)
@@ -156,6 +156,7 @@
 
 
 ROW = 4
+QUARTERS = 4
 STEPS = (2, 1, 3, 0)
 
 
@@ -241,24 +242,33 @@
     trade.finish(0)
 
 
-def inverse_kernel(sources, arrived, legendre, factor, ens_hbm, modes_ref, out_ref,
-                   landing, packed, lift_ref, ens, table, turn, turned, fields, mine, theirs,
-                   load_sem, mem_send, mem_recv, *sems):
+def inverse_kernel(sources, arrived_hbm, legendre_hbm, factor, ens_hbm, modes_ref, out_ref,
+                   arrived, legendre, landing, packed, lift_ref, ens, table, turn, turned, fields, mine, theirs,
+                   load_sem, first_sem, mem_send, mem_recv, *sems):
     own_waves = legendre.shape[0]
     members, levels, lat_rows = ens.shape[:3]
     groups = lat_rows // TILE
     eight = TILE // 2
     half = LANES // 2
-    middle = own_waves // 2
+    few = own_waves // QUARTERS
     width = mine.shape[2]
     pieces = NLON // width
     load = pltpu.make_async_copy(ens_hbm, ens, load_sem.at[0])
+    firsts = []
+    for q in range(QUARTERS):
+        own, pair = pl.ds(q * few, few), pl.ds(2 * q * few, 2 * few)
+        firsts.append((
+            pltpu.make_async_copy(arrived_hbm.at[:, pair], arrived.at[:, pair], first_sem.at[0, q]),
+            pltpu.make_async_copy(legendre_hbm.at[own], legendre.at[own], first_sem.at[1, q]),
+        ))
+        for first in firsts[q]:
+            first.start()
     load.start()
 
     trade = Exchange(
         sources,
-        lambda step, i, part: packed.at[trade.device(step, i), part // 2, pl.ds(part % 2 * middle, middle)],
-        lambda source, part: landing.at[source, part // 2, pl.ds(part % 2 * middle, middle)],
+        lambda step, i, part: packed.at[trade.device(step, i), part // QUARTERS, pl.ds(part % QUARTERS * few, few)],
+        lambda source, part: landing.at[source, part // QUARTERS, pl.ds(part % QUARTERS * few, few)],
         *sems,
     )
     other = 1 - lax.axis_index("mem")
@@ -280,19 +290,21 @@
         parts = [synthesis[:, r * LANES : (r + 1) * LANES].reshape(sources, groups, eight, LANES) for r in range(2)]
         packed[:, :, m] = jnp.concatenate(parts, axis=2).astype(BF16)
 
-    pl.loop(0, middle)(wave)
-    for step in STEPS:
-        trade.start(step, 0)
-    pl.loop(middle, own_waves)(wave)
-    for part in (1, 2, 3):
+    for q in range(QUARTERS):
+        for first in firsts[q]:
+            first.wait()
+        pl.loop(q * few, (q + 1) * few)(wave)
+        for step in STEPS:
+            trade.start(step, q)
+    for part in range(QUARTERS, groups * QUARTERS):
         for step in STEPS:
             trade.start(step, part)
     lift_ref[...] = spread_modes(modes_ref, levels, False)
     build_table(table, True)
     load.wait()
     for g in range(groups):
-        trade.finish(2 * g)
-        trade.finish(2 * g + 1)
+        for q in range(QUARTERS):
+            trade.finish(g * QUARTERS + q)
 
         @pl.loop(0, sources)
         def _(source):
@@ -341,7 +353,6 @@
     own_waves = legendre.shape[0]
     sources = lax.axis_size("space")
     share = 2 * own_waves
-    narrow = modes.astype(BF16)
     wavenumber = (
         lax.axis_index("space") * own_waves
         + jnp.arange(own_waves, dtype=jnp.int32)[:, None]
@@ -375,15 +386,17 @@
         ],
         compiler_params=params(0),
         name="forward",
-    )(ensemble, vector, narrow)
+    )(ensemble, vector, modes)
     traded = pltpu.VMEM((sources, groups, own_waves, TILE, LANES), BF16)
-    parts = 2 * groups
+    parts = QUARTERS * groups
     return pl.pallas_call(
         lambda *refs: inverse_kernel(sources, *refs),
         out_shape=jax.ShapeDtypeStruct(vector.shape, BF16),
-        in_specs=[vmem, vmem, vmem, any_space, vmem],
+        in_specs=[any_space, any_space, vmem, any_space, vmem],
         out_specs=vmem,
         scratch_shapes=[
+            pltpu.VMEM(exchanged.shape, BF16),
+            pltpu.VMEM(legendre.shape, BF16),
             traded,
             traded,
             pltpu.VMEM((levels * TILE, TILE * NMODE), BF16),
@@ -395,6 +408,7 @@
             pltpu.VMEM((pieces, levels * TILE, width), BF16),
             pltpu.VMEM((pieces, levels * TILE, width), BF16),
             dma((1,)),
+            dma((2, QUARTERS)),
             dma((pieces,)),
             dma((pieces,)),
             dma((parts,)),
@@ -403,7 +417,7 @@
         ],
         compiler_params=params(1),
         name="inverse",
-    )(arrived, legendre, factor, ensemble, narrow)
+    )(arrived, legendre, factor, ensemble, modes)
 
 
 def on_device(ensemble, vector, modes, legendre, spectrum, truncation):

time: 280 us -> 273 us (0.975)
  Pallas kernels: 272 us -> 265 us
    pallas_call x1, Pallas kernels: 159 us -> 153 us  [kernel_path(): pl.pallas_call(lambda *refs: inverse_kernel(sources, *refs), out_shape=ja...]
where the time goes in v3:
time: 273 us; the launch traced here: 271 us
  Pallas kernels  265 us (97%)
  local copies, waits for them, and re-layouts  3.88 us (1%)
    pallas_call x1, Pallas kernels, kernel_path(): pl.pallas_call(lambda *refs: inverse_kernel(sources, *refs), out_shape=ja...  153 us
    pallas_call x1, Pallas kernels, kernel_path(): pl.pallas_call(lambda *refs: forward_kernel(sources, *refs), out_shape=ex...  112 us

profile of v3, /device:TPU:15, one launch (start us, length us, event | category | flops | bytes accessed | tf_op | source)
XLA Modules:
  0.0 271.4 jit_solution(5563100943292761486)
XLA Ops:
  0.7 1.4 fusion.refs_2_
  2.1 112.4 %forward.1.refs_0_ = bf16[16,64,16,128]{3,2,1,0:T(8,128)(2,1)} custom-call(bf16[4,32,32,1536]{3,2,1,0:T(8,128)(2,1)} %refs_3_.1, bf16[32,32,1536]{2,1,0:T(8,128)(2,1)} %refs_1_.2, f32[16,32]{1,0:T(8,128)} %refs_4_.1), custom_call_target="tpu_custom_call" | custom-call | tf_op jit(solution)/shard_map/forward/pallas_call | solution.py:369
  114.5 153.1 %inverse.1 = bf16[32,32,1536]{2,1,0:T(8,128)(2,1)} custom-call(bf16[16,64,16,128]{3,2,1,0:T(8,128)(2,1)} %forward.1.refs_0_, bf16[32,512,256]{2,1,0:T(8,128)(2,1)} %refs_1_.3, f32[32,256]{1,0:T(8,128)} %fusion.refs_2_, bf16[4,32,32,1536]{3,2,1,0:T(8,128)(2,1)} %refs_3_.1, f32[16,32]{1,0:T(8,128)} %refs_4_.1), custom_call_target="tpu_custom_call" | custom-call | tf_op jit(solution)/shard_map/inverse/pallas_call | solution.py:392
  267.5 3.9 %copy.9 = bf16[32,32,1536]{2,1,0:T(8,128)(2,1)} copy(bf16[32,32,1536]{2,1,0:T(8,128)(2,1)} %inverse.1) | data formatting | bytes 6291456
  (1 shorter events, 0.0 us)
